TPU v7x, 32 devices: a whole 2x2x4 slice. The times are simulated.
32 devices in a mesh: seq: 8 (over z, x), head: 4 (over y, core).
Axes of the slice: x: 2, y: 2, z: 4, core: 2. Of those that a mesh axis runs over, the one named last changes fastest.
Arguments:
- inputs: bfloat16 [3, 4096, 4096], P(None, 'seq', 'head'), may hold values from -11 to 11
- conv_weight: float32 [3, 3, 4096], P(None, None, 'head'), may hold values from -9 to 9
- gain: float32 [4096], P('head'), may hold values from 0.5 to 1.5
- cotangent: bfloat16 [4096, 4096], P('seq', 'head'), may hold values from -11 to 11
Outputs:
- output: bfloat16 [4096, 4096], P('seq', 'head')
- grad_inputs: bfloat16 [3, 4096, 4096], P(None, 'seq', 'head')
All inputs are finite; a program needn't handle non-finite values.
Results may differ from a plain program's by a relative error of at most 0.0078.
Values may be sent and summed in bfloat16 or wider, within the bound.
A program may use at most 128 MiB of HBM per device.

v0:
```python
import jax
import jax.numpy as jnp
from jax import lax
from jax.sharding import PartitionSpec as P

WIDTH = 4096
HEAD_DIM = 128
BLOCK = 512


def from_behind(x, axis, by):
    devices = lax.axis_size(axis)
    pairs = [(i, i + by) for i in range(devices) if 0 <= i + by < devices]
    return lax.ppermute(x, axis, pairs)


def entering(part, axis, combine, identity, reverse):
    count = lax.axis_size(axis)
    place = lax.axis_index(axis)
    ahead = count - 1 - place if reverse else place
    gathered = lax.all_gather(part, axis)
    state = jnp.zeros_like(part) + jnp.asarray(identity, part.dtype)

    def one(step, state):
        source = count - 1 - step if reverse else step
        return combine(state, lax.dynamic_index_in_dim(gathered, source, 0, False))

    return lax.fori_loop(0, ahead, one, state)


def add_states(earlier, later):
    return earlier + later


def body(inputs, conv_weight, gain, cotangent):
    row_count = inputs.shape[1]
    col_count = inputs.shape[2]
    tap_count = conv_weight.shape[1]
    local_heads = col_count // HEAD_DIM
    block_count = row_count // BLOCK
    left_rim = from_behind(inputs[:, row_count - (tap_count - 1) :, :], "seq", 1)
    extended = jnp.concatenate([left_rim, inputs], axis=1).astype(jnp.float32)
    conv_total = jnp.zeros((3, row_count, col_count), jnp.float32)
    for offset in range(tap_count):
        start_row = tap_count - 1 - offset
        conv_total = (
            conv_total
            + conv_weight[:, offset, None, :] * extended[:, start_row : start_row + row_count, :]
        )
    convolved = conv_total.astype(jnp.bfloat16)

    def by_blocks(array):
        return array.reshape(block_count, BLOCK, local_heads, HEAD_DIM)

    queries = by_blocks(convolved[0])
    key_rows = by_blocks(convolved[1])
    values = by_blocks(convolved[2])
    causal = lax.broadcasted_iota(jnp.int32, (BLOCK, BLOCK), 0) >= lax.broadcasted_iota(
        jnp.int32, (BLOCK, BLOCK), 1
    )
    block_states = jnp.einsum(
        "nshd,nshe->nhde", key_rows, values, preferred_element_type=jnp.float32
    )
    device_state = jnp.sum(block_states, axis=0)
    zero_state = jnp.zeros_like(device_state)
    incoming = entering(device_state, "seq", add_states, zero_state, False)
    state = incoming[None] + jnp.cumsum(block_states, axis=0) - block_states
    state_bf = state.astype(jnp.bfloat16)
    scores = jnp.einsum("nthd,nshd->nhts", queries, key_rows, preferred_element_type=jnp.float32)
    scores = jnp.where(causal[None, None], scores, 0.0).astype(jnp.bfloat16)
    attended = jnp.einsum("nthd,nhde->nthe", queries, state_bf, preferred_element_type=jnp.float32)
    attended = attended + jnp.einsum(
        "nhts,nshe->nthe", scores, values, preferred_element_type=jnp.float32
    )
    attended = attended.reshape(row_count, col_count)
    weighted = gain[None, :] * cotangent.astype(jnp.float32)
    squares = jnp.sum(attended * attended, axis=-1)
    total_sq = lax.psum(squares, "head")
    rms = jnp.sqrt(total_sq / WIDTH + 1e-05)
    output = (gain[None, :] * attended / rms[:, None]).astype(jnp.bfloat16)
    inner = lax.psum(jnp.sum(weighted * attended, axis=-1), "head")
    grad_attended = (
        weighted / rms[:, None] - attended * (inner / (WIDTH * rms * rms * rms))[:, None]
    ).astype(jnp.bfloat16)
    grad_blocks = by_blocks(grad_attended)
    block_grads = jnp.einsum(
        "nthd,nthe->nhde", queries, grad_blocks, preferred_element_type=jnp.float32
    )
    device_grad = jnp.sum(block_grads, axis=0)
    later_grad = entering(device_grad, "seq", add_states, zero_state, True)
    after = later_grad[None] + device_grad[None] - jnp.cumsum(block_grads, axis=0)
    after_bf = after.astype(jnp.bfloat16)
    mixed = jnp.einsum("nthe,nshe->nhts", grad_blocks, values, preferred_element_type=jnp.float32)
    mixed = jnp.where(causal[None, None], mixed, 0.0).astype(jnp.bfloat16)
    grad_q = jnp.einsum(
        "nthe,nhde->nthd", grad_blocks, state_bf, preferred_element_type=jnp.float32
    )
    grad_q = grad_q + jnp.einsum(
        "nhts,nshd->nthd", mixed, key_rows, preferred_element_type=jnp.float32
    )
    grad_k = jnp.einsum("nshe,nhde->nshd", values, after_bf, preferred_element_type=jnp.float32)
    grad_k = grad_k + jnp.einsum(
        "nhts,nthd->nshd", mixed, queries, preferred_element_type=jnp.float32
    )
    grad_v = jnp.einsum("nshd,nhde->nshe", key_rows, after_bf, preferred_element_type=jnp.float32)
    grad_v = grad_v + jnp.einsum(
        "nhts,nthe->nshe", scores, grad_blocks, preferred_element_type=jnp.float32
    )
    grad_u = (
        jnp.stack([grad_q, grad_k, grad_v]).reshape(3, row_count, col_count).astype(jnp.bfloat16)
    )
    right_rim = from_behind(grad_u[:, : tap_count - 1, :], "seq", -1)
    extended_grad = jnp.concatenate([grad_u, right_rim], axis=1).astype(jnp.float32)
    grad_total_in = jnp.zeros((3, row_count, col_count), jnp.float32)
    for offset in range(tap_count):
        grad_total_in = (
            grad_total_in
            + conv_weight[:, offset, None, :] * extended_grad[:, offset : offset + row_count, :]
        )
    return (output, grad_total_in.astype(jnp.bfloat16))


def solution(mesh):
    placed = (P(None, "seq", "head"), P(None, None, "head"), P("head"), P("seq", "head"))
    return jax.shard_map(
        body,
        mesh=mesh,
        in_specs=placed,
        out_specs=(P("seq", "head"), P(None, "seq", "head")),
        check_vma=False,
    )
```

profile of v0, /device:TPU:0, one launch (start us, length us, event | category | flops | bytes accessed | tf_op | source)
XLA Modules:
  0.0 241.4 jit_solution(3161101124645385469)
XLA Ops:
  8.0 4.9 %collective-permute-start = (bf16[3,2,1024]{2,1,0:T(2,128)(2,1)S(1)}, bf16[3,2,1024]{2,1,0:T(2,128)(2,1)S(1)}, u32[]{:S(2)}, u32[]{:S(2)}) collective-permute-start(bf16[3,2,1024]{2,1,0:T(2,128)(2,1)S(1)} %slice.46), channel_id=1, source_target_pairs={{0,4},{4,8},{8,12},{12,16},{16,20},{20,24},{24,28},{1,5},{5,9},{9,... | collective-permute-start | bytes 36872 | tf_op jit(solution)/shard_map/ppermute | solution.py:14
  13.9 4.6 %copy.44 = bf16[3,512,1024]{1,2,0:T(8,128)(2,1)} copy(bf16[3,512,1024]{2,1,0:T(8,128)(2,1)} %param.8) | data formatting | bytes 6291456 | tf_op args[0]
  18.9 3.6 %maximum_convert_fusion = f32[3,514,1024]{1,2,0:T(8,128)S(1)} fusion(bf16[3,512,1024]{1,2,0:T(8,128)(2,1)} %copy.44, bf16[3,2,1024]{1,2,0:T(8,128)(2,1)S(1)} %copy.43), kind=kLoop, calls=%fused_computation.16 | loop fusion | flops 6316032 | bytes 9474048 | tf_op jit(solution)/shard_map/convert_element_type | solution.py:42
  22.5 5.7 %fusion.4 = bf16[3,512,1024]{1,2,0:T(8,128)(2,1)S(1)} fusion(f32[3,514,1024]{1,2,0:T(8,128)S(1)} %maximum_convert_fusion, f32[3,1024]{1,0:T(4,128)S(1)} %get-tuple-element.117, f32[3,1024]{1,0:T(4,128)S(1)} %get-tuple-element.118, f32[3,1024]{1,0:T(4,128)S(1)} %bitcast.93), kind=kLoop, calls=%fused_computation.12 | loop fusion | flops 9437184 | bytes 22056960 | tf_op jit(solution)/shard_map/convert_element_type | solution.py:50
  32.2 1.9 copy-done
  34.2 2.8 %fusion.13 = f32[8,128,512]{2,1,0:T(8,128)} fusion(bf16[512,8,128]{0,2,1:T(8,128)(2,1)S(1)} %bitcast.73, bf16[8,512,512]{2,1,0:T(8,128)(2,1)S(1)} %select_convert_fusion.1), kind=kOutput, calls=%fused_computation.44 | convolution fusion | flops 536870912 | bytes 7340032 | tf_op jit(solution)/shard_map/nhts,nshe->nthe/dot_general | solution.py:72
  37.0 66.3 %all-gather.5.cloned.1.call-done = f32[64,128,128]{2,1,0:T(8,128)} async-done(((f32[8,128,128]{2,1,0:T(8,128)}), f32[64,128,128]{2,1,0:T(8,128)}) %all-gather.5.cloned.1.call-update) | async-done | bytes 4194320 | tf_op jit(solution)/shard_map/all_gather | solution.py:21
  104.4 3.4 %fusion.6 = (f32[512]{0:T(512)S(1)}, f32[8,128,512]{2,1,0:T(8,128)}) fusion(f32[8,128,512]{2,1,0:T(8,128)} %fusion.13, bf16[8,128,128]{2,1,0:T(8,128)(2,1)S(1)} %fusion.7, bf16[512,8,128]{0,2,1:T(8,128)(2,1)S(1)} %bitcast.81), kind=kOutput, calls=%fused_computation.19 | convolution fusion | flops 135790080 | bytes 5507072 | tf_op jit(solution)/shard_map/nthd,nhde->nthe/dot_general | solution.py:71
  107.8 1.9 copy.50
  109.7 1.6 multiply_reduce_fusion
  111.3 5.8 %all-reduce = (f32[512]{0:T(512)S(1)}, f32[512]{0:T(512)S(1)}) all-reduce(f32[512]{0:T(512)S(1)} %get-tuple-element.115, f32[512]{0:T(512)S(1)} %multiply_reduce_fusion), channel_id=1, replica_groups=mesh['seq'=8,'head'=4] {'head'}, use_global_device_ids=true, to_apply=%region_3.4 | all-reduce | flops 1024 | bytes 8192 | tf_op jit(solution)/shard_map/psum | solution.py:78
  117.2 3.2 %subtract_convert_fusion = (bf16[512,1024]{1,0:T(8,128)(2,1)}, bf16[512,1024]{1,0:T(8,128)(2,1)}) fusion(f32[512,1024]{1,0:T(8,128)S(1)} %copy.50, bf16[512,1024]{1,0:T(8,128)(2,1)} %param.11, f32[512]{0:T(512)S(1)} %get-tuple-element.113, f32[512]{0:T(512)S(1)} %get-tuple-element.114, f32[1024]{0:T(1024)S(1)} %copy-done.12), kind=kLoop, calls=%fused_computation.23 | loop fusion | flops 4718592 | bytes 5251072 | tf_op jit(solution)/shard_map/convert_element_type | solution.py:84
  120.3 1.5 copy.76
  121.8 2.5 %fusion.15 = f32[8,128,128]{2,1,0:T(8,128)} fusion(bf16[512,8,128]{0,2,1:T(8,128)(2,1)} %bitcast.82, bf16[512,8,128]{0,2,1:T(8,128)(2,1)S(1)} %bitcast.68), kind=kOutput, calls=%fused_computation.46 | convolution fusion | flops 134217728 | bytes 2621440 | tf_op jit(solution)/shard_map/nthd,nthe->nhde/dot_general | solution.py:86
  124.3 2.4 select_convert_fusion
  129.6 2.0 fusion.17
  131.7 2.1 fusion.16
  133.8 69.7 %all-gather.7.cloned.1.call-done = f32[64,128,128]{2,1,0:T(8,128)} async-done(((f32[8,128,128]{2,1,0:T(8,128)}), f32[64,128,128]{2,1,0:T(8,128)}) %all-gather.7.cloned.1.call-update) | async-done | bytes 4194320 | tf_op jit(solution)/shard_map/all_gather | solution.py:21
  203.5 8.4 %while.23 = (s32[]{:T(128)}, f32[8,128,128]{2,1,0:T(8,128)S(1)}, s32[]{:T(128)}, f32[8,8,128,128]{3,2,1,0:T(8,128)}, s32[]{:T(128)}, /*index=5*/s32[]{:T(128)}, s32[]{:T(128)}, s32[]{:T(128)}) while((s32[]{:T(128)}, f32[8,128,128]{2,1,0:T(8,128)S(1)}, s32[]{:T(128)}, f32[8,8,128,128]{3,2,1,0:T(8,128)}, s32[]{:T(128)}, /*index=5*/s32[]{:T(128)}, ...), condition=%wide.region_7.8_spmd, body=%wide.region_6.7_spmd.sunk | while | flops 131078 | bytes 1573007 | solution.py:28
  212.0 2.2 add_convert_fusion
  217.0 4.3 %collective-permute-done.1 = bf16[3,2,1024]{2,1,0:T(2,128)(2,1)S(1)} collective-permute-done((bf16[3,2,1024]{2,1,0:T(2,128)(2,1)S(1)}, bf16[3,2,1024]{2,1,0:T(2,128)(2,1)S(1)}, u32[]{:S(2)}, u32[]{:S(2)}) %collective-permute-start.1) | collective-permute-done | bytes 12320 | tf_op jit(solution)/shard_map/ppermute | solution.py:14
  221.7 1.6 maximum_convert_fusion.1
  223.3 6.7 %fusion.1 = bf16[3,512,1024]{1,2,0:T(8,128)(2,1)} fusion(f32[3,514,1024]{1,2,0:T(8,128)S(1)} %maximum_convert_fusion.1, f32[3,1024]{1,0:T(4,128)S(1)} %get-tuple-element.117, f32[3,1024]{1,0:T(4,128)S(1)} %get-tuple-element.118, f32[3,1024]{1,0:T(4,128)S(1)} %bitcast.94), kind=kLoop, calls=%fused_computation.6 | loop fusion | flops 9437184 | bytes 22056960 | tf_op jit(solution)/shard_map/convert_element_type | solution.py:120
  229.9 4.6 %copy.63 = bf16[3,512,1024]{2,1,0:T(8,128)(2,1)} copy(bf16[3,512,1024]{1,2,0:T(8,128)(2,1)} %fusion.1) | data formatting | bytes 6291456
  (59 shorter events, 21.6 us)
Async XLA Ops:
  7.2 96.1 %all-gather.5.cloned.1.call-start = ((), (), s32[]{:S(2)}) async-start(), calls=%async_computation | async-start | bytes 4718592 | tf_op jit(solution)/shard_map/all_gather | solution.py:21
  8.0 10.5 %collective-permute-start = (bf16[3,2,1024]{2,1,0:T(2,128)(2,1)S(1)}, bf16[3,2,1024]{2,1,0:T(2,128)(2,1)S(1)}, u32[]{:S(2)}, u32[]{:S(2)}) collective-permute-start(bf16[3,2,1024]{2,1,0:T(2,128)(2,1)S(1)} %slice.46), channel_id=1, source_target_pairs={{0,4},{4,8},{8,12},{12,16},{16,20},{20,24},{24,28},{1,5},{5,9},{9,... | collective-permute-start | bytes 36872 | tf_op jit(solution)/shard_map/ppermute | solution.py:14
  28.5 3.7 %copy-start.2 = (bf16[1,512,1024]{1,2,0:T(8,128)(2,1)}, bf16[1,512,1024]{1,2,0:T(8,128)(2,1)S(1)}, u32[]{:S(2)}) copy-start(bf16[1,512,1024]{1,2,0:T(8,128)(2,1)S(1)} %get-tuple-element.105) | copy-start | bytes 3145732
  28.5 75.9 %copy-start.4 = (bf16[1,512,1024]{1,2,0:T(8,128)(2,1)}, bf16[1,512,1024]{1,2,0:T(8,128)(2,1)S(1)}, u32[]{:S(2)}) copy-start(bf16[1,512,1024]{1,2,0:T(8,128)(2,1)S(1)} %get-tuple-element.106) | copy-start | bytes 3145732
  30.0 173.5 %all-gather.7.cloned.1.call-start = ((), (), s32[]{:S(2)}) async-start(), calls=%async_computation.1 | async-start | bytes 4718592 | tf_op jit(solution)/shard_map/all_gather | solution.py:21
  30.1 0.7 copy-start.11
  32.2 1.9 copy-start
  103.3 1.0 copy-start.10
  104.4 5.3 %copy-start.12 = (f32[1024]{0:T(1024)S(1)}, f32[1024]{0:T(1024)}, u32[]{:S(2)}) copy-start(f32[1024]{0:T(1024)} %param.10) | copy-start | bytes 12292
  124.3 2.4 %copy-start.3 = (bf16[1,512,1024]{1,2,0:T(8,128)(2,1)S(1)}, bf16[1,512,1024]{1,2,0:T(8,128)(2,1)}, u32[]{:S(2)}) copy-start(bf16[1,512,1024]{1,2,0:T(8,128)(2,1)} %copy-done.2) | copy-start | bytes 3145732
  126.7 2.9 %copy-start.1 = (bf16[8,512,512]{2,1,0:T(8,128)(2,1)S(1)}, bf16[8,512,512]{2,1,0:T(8,128)(2,1)}, u32[]{:S(2)}) copy-start(bf16[8,512,512]{2,1,0:T(8,128)(2,1)} %copy-done) | copy-start | bytes 12582916
  129.6 2.1 copy-start.5
  203.5 8.5 %copy-start.9 = (f32[8,128,128]{2,1,0:T(8,128)S(1)}, f32[8,128,128]{2,1,0:T(8,128)}, u32[]{:S(2)}) copy-start(f32[8,128,128]{2,1,0:T(8,128)} %fusion.15) | copy-start | bytes 1572868
  211.9 2.3 copy-start.8
  212.0 3.2 %copy-start.6 = (bf16[8,128,512]{2,1,0:T(8,128)(2,1)S(1)}, bf16[8,128,512]{2,1,0:T(8,128)(2,1)}, u32[]{:S(2)}) copy-start(bf16[8,128,512]{2,1,0:T(8,128)(2,1)} %add_convert_fusion.2) | copy-start | bytes 3145732
  214.2 1.0 copy-start.7
  215.7 5.6 %collective-permute-start.1 = (bf16[3,2,1024]{2,1,0:T(2,128)(2,1)S(1)}, bf16[3,2,1024]{2,1,0:T(2,128)(2,1)S(1)}, u32[]{:S(2)}, u32[]{:S(2)}) collective-permute-start(bf16[3,2,1024]{2,1,0:T(2,128)(2,1)S(1)} %copy.61), channel_id=1, source_target_pairs={{4,0},{8,4},{12,8},{16,12},{20,16},{24,20},{28,24},{5,1},{9,5},{13... | collective-permute-start | bytes 36872 | tf_op jit(solution)/shard_map/ppermute | solution.py:14
Sparse Core Ops, SparseCore 0:
  30.1 73.0 all-gather.4
  124.4 78.9 all-gather.6
where the time goes:
time: 242 us; the launch traced here: 241 us
  waiting for transfers between devices  140 us (58%)
  other arithmetic  30.9 us (13%)
  matrix products  23.6 us (10%)
  local copies, waits for them, and re-layouts  20 us (8%)
  between operations  14.3 us (6%)
  starting transfers between devices  6.24 us (3%)
  blocking collectives  5.85 us (2%)
    all_gather x2, waiting for transfers between devices, entering(): gathered = lax.all_gather(part, axis)  136 us
    unnamed x30, local copies, waits for them, and re-layouts  13.4 us
    add x7, other arithmetic, add_states(): return earlier + later  8.23 us
    convert_element_type x1, other arithmetic, body(): return (output, grad_total_in.astype(jnp.bfloat16))  6.65 us
    ppermute x2, starting transfers between devices, from_behind(): return lax.ppermute(x, axis, pairs)  6.16 us
    psum x1, blocking collectives, body(): total_sq = lax.psum(squares, 'head')  5.85 us
    convert_element_type x1, other arithmetic, body(): convolved = conv_total.astype(jnp.bfloat16)  5.72 us
  transfers between devices with their start and end apart: 4, of which 3 were waited for; matrix products, arithmetic and copies ran while one was open for 8% of the time, Pallas kernels for 0%

commit v1 on v0

--- a/solution.py
+++ b/solution.py
@@ -6,6 +6,10 @@
 WIDTH = 4096
 HEAD_DIM = 128
 BLOCK = 512
+
+
+def _fit_lane(frame):
+    return jnp.sum(jax.lax.all_gather(frame, "head"), axis=0)
 
 
 def from_behind(x, axis, by):
@@ -75,7 +79,7 @@
     attended = attended.reshape(row_count, col_count)
     weighted = gain[None, :] * cotangent.astype(jnp.float32)
     squares = jnp.sum(attended * attended, axis=-1)
-    total_sq = lax.psum(squares, "head")
+    total_sq = _fit_lane(squares)
     rms = jnp.sqrt(total_sq / WIDTH + 1e-05)
     output = (gain[None, :] * attended / rms[:, None]).astype(jnp.bfloat16)
     inner = lax.psum(jnp.sum(weighted * attended, axis=-1), "head")

time: 242 us -> 248 us (1.025)
  blocking collectives: 5.85 us -> 11 us
    all_gather x0 -> x1, blocking collectives: none -> 5.36 us  [_fit_lane(): return jnp.sum(jax.lax.all_gather(frame, 'head'), axis=0)]
where the time goes in v1:
time: 248 us; the launch traced here: 247 us
  waiting for transfers between devices  140 us (56%)
  other arithmetic  30.9 us (12%)
  matrix products  23.6 us (10%)
  local copies, waits for them, and re-layouts  20 us (8%)
  between operations  14.3 us (6%)
  blocking collectives  11 us (4%)
  starting transfers between devices  6.24 us (3%)
    all_gather x2, waiting for transfers between devices, entering(): gathered = lax.all_gather(part, axis)  136 us
    unnamed x30, local copies, waits for them, and re-layouts  13.5 us
    add x7, other arithmetic, add_states(): return earlier + later  8.23 us
    convert_element_type x1, other arithmetic, body(): return (output, grad_total_in.astype(jnp.bfloat16))  6.64 us
    ppermute x2, starting transfers between devices, from_behind(): return lax.ppermute(x, axis, pairs)  6.16 us
    convert_element_type x1, other arithmetic, body(): convolved = conv_total.astype(jnp.bfloat16)  5.72 us
    psum x1, blocking collectives, body(): inner = lax.psum(jnp.sum(weighted * attended, axis=-1), 'head')  5.66 us
    all_gather x1, blocking collectives, _fit_lane(): return jnp.sum(jax.lax.all_gather(frame, 'head'), axis=0)  5.36 us
  transfers between devices with their start and end apart: 4, of which 3 were waited for; matrix products, arithmetic and copies ran while one was open for 8% of the time, Pallas kernels for 0%

profile of v1, /device:TPU:0, one launch (start us, length us, event | category | flops | bytes accessed | tf_op | source)
XLA Modules:
  0.0 246.6 jit_solution(17428833264811282642)
XLA Ops:
  8.0 4.9 %collective-permute-start = (bf16[3,2,1024]{2,1,0:T(2,128)(2,1)S(1)}, bf16[3,2,1024]{2,1,0:T(2,128)(2,1)S(1)}, u32[]{:S(2)}, u32[]{:S(2)}) collective-permute-start(bf16[3,2,1024]{2,1,0:T(2,128)(2,1)S(1)} %slice.46), channel_id=1, source_target_pairs={{0,4},{4,8},{8,12},{12,16},{16,20},{20,24},{24,28},{1,5},{5,9},{9,... | collective-permute-start | bytes 36872 | tf_op jit(solution)/shard_map/ppermute | solution.py:18
  13.9 4.6 %copy.44 = bf16[3,512,1024]{1,2,0:T(8,128)(2,1)} copy(bf16[3,512,1024]{2,1,0:T(8,128)(2,1)} %param.8) | data formatting | bytes 6291456 | tf_op args[0]
  18.9 3.6 %maximum_convert_fusion = f32[3,514,1024]{1,2,0:T(8,128)S(1)} fusion(bf16[3,512,1024]{1,2,0:T(8,128)(2,1)} %copy.44, bf16[3,2,1024]{1,2,0:T(8,128)(2,1)S(1)} %copy.43), kind=kLoop, calls=%fused_computation.16 | loop fusion | flops 6316032 | bytes 9474048 | tf_op jit(solution)/shard_map/convert_element_type | solution.py:46
  22.5 5.7 %fusion.4 = bf16[3,512,1024]{1,2,0:T(8,128)(2,1)S(1)} fusion(f32[3,514,1024]{1,2,0:T(8,128)S(1)} %maximum_convert_fusion, f32[3,1024]{1,0:T(4,128)S(1)} %get-tuple-element.115, f32[3,1024]{1,0:T(4,128)S(1)} %get-tuple-element.116, f32[3,1024]{1,0:T(4,128)S(1)} %bitcast.94), kind=kLoop, calls=%fused_computation.12 | loop fusion | flops 9437184 | bytes 22056960 | tf_op jit(solution)/shard_map/convert_element_type | solution.py:54
  32.2 2.0 copy-done
  34.2 2.8 %fusion.13 = f32[8,128,512]{2,1,0:T(8,128)} fusion(bf16[512,8,128]{0,2,1:T(8,128)(2,1)S(1)} %bitcast.74, bf16[8,512,512]{2,1,0:T(8,128)(2,1)S(1)} %select_convert_fusion.1), kind=kOutput, calls=%fused_computation.44 | convolution fusion | flops 536870912 | bytes 7340032 | tf_op jit(solution)/shard_map/nhts,nshe->nthe/dot_general | solution.py:76
  37.0 66.3 %all-gather.7.cloned.1.call-done = f32[64,128,128]{2,1,0:T(8,128)} async-done(((f32[8,128,128]{2,1,0:T(8,128)}), f32[64,128,128]{2,1,0:T(8,128)}) %all-gather.7.cloned.1.call-update) | async-done | bytes 4194320 | tf_op jit(solution)/shard_map/all_gather | solution.py:25
  104.4 3.4 %fusion.6 = (f32[512]{0:T(512)S(1)}, f32[8,128,512]{2,1,0:T(8,128)}) fusion(f32[8,128,512]{2,1,0:T(8,128)} %fusion.13, bf16[8,128,128]{2,1,0:T(8,128)(2,1)S(1)} %fusion.7, bf16[512,8,128]{0,2,1:T(8,128)(2,1)S(1)} %bitcast.82), kind=kOutput, calls=%fused_computation.19 | convolution fusion | flops 135790080 | bytes 5507072 | tf_op jit(solution)/shard_map/nthd,nhde->nthe/dot_general | solution.py:75
  107.8 1.9 copy.50
  109.7 1.6 multiply_reduce_fusion
  111.3 5.7 %psum.7 = f32[512]{0:T(512)S(1)} all-reduce(f32[512]{0:T(512)S(1)} %multiply_reduce_fusion), channel_id=1, replica_groups=mesh['seq'=8,'head'=4] {'head'}, use_global_device_ids=true, to_apply=%region_5.6 | all-reduce | flops 512 | bytes 4096 | tf_op jit(solution)/shard_map/psum | solution.py:85
  117.0 5.4 %all-gather.3 = f32[4,1,512]{2,1,0:T(1,128)S(1)} all-gather(f32[1,1,512]{2,1,0:T(1,128)S(1)} %bitcast.96), channel_id=3, replica_groups=mesh['seq'=8,'head'=4] {'head'}, dimensions={0}, use_global_device_ids=true | all-gather | bytes 10240 | tf_op jit(solution)/shard_map/all_gather | solution.py:12
  122.4 3.2 %subtract_convert_fusion = (bf16[512,1024]{1,0:T(8,128)(2,1)}, bf16[512,1024]{1,0:T(8,128)(2,1)}) fusion(f32[512,1024]{1,0:T(8,128)S(1)} %copy.50, bf16[512,1024]{1,0:T(8,128)(2,1)} %param.11, f32[512]{0:T(512)S(1)} %get-tuple-element.111, f32[512]{0:T(512)S(1)} %get-tuple-element.112, f32[1024]{0:T(1024)S(1)} %copy-done.12), kind=kLoop, calls=%fused_computation.23 | loop fusion | flops 4718592 | bytes 5251072 | tf_op jit(solution)/shard_map/convert_element_type | solution.py:88
  127.1 2.5 fusion.15
  129.5 2.4 select_convert_fusion
  134.9 2.0 fusion.17
  136.9 2.1 fusion.16
  139.0 69.7 %all-gather.9.cloned.1.call-done = f32[64,128,128]{2,1,0:T(8,128)} async-done(((f32[8,128,128]{2,1,0:T(8,128)}), f32[64,128,128]{2,1,0:T(8,128)}) %all-gather.9.cloned.1.call-update) | async-done | bytes 4194320 | tf_op jit(solution)/shard_map/all_gather | solution.py:25
  208.7 8.4 %while.23 = (s32[]{:T(128)}, f32[8,128,128]{2,1,0:T(8,128)S(1)}, s32[]{:T(128)}, f32[8,8,128,128]{3,2,1,0:T(8,128)}, s32[]{:T(128)}, /*index=5*/s32[]{:T(128)}, s32[]{:T(128)}, s32[]{:T(128)}) while((s32[]{:T(128)}, f32[8,128,128]{2,1,0:T(8,128)S(1)}, s32[]{:T(128)}, f32[8,8,128,128]{3,2,1,0:T(8,128)}, s32[]{:T(128)}, /*index=5*/s32[]{:T(128)}, ...), condition=%wide.region_7.8_spmd, body=%wide.region_6.7_spmd.sunk | while | flops 131078 | bytes 1573007 | solution.py:32
  217.2 2.2 add_convert_fusion
  222.2 4.3 %collective-permute-done.1 = bf16[3,2,1024]{2,1,0:T(2,128)(2,1)S(1)} collective-permute-done((bf16[3,2,1024]{2,1,0:T(2,128)(2,1)S(1)}, bf16[3,2,1024]{2,1,0:T(2,128)(2,1)S(1)}, u32[]{:S(2)}, u32[]{:S(2)}) %collective-permute-start.1) | collective-permute-done | bytes 12320 | tf_op jit(solution)/shard_map/ppermute | solution.py:18
  226.9 1.6 maximum_convert_fusion.1
  228.5 6.6 %fusion.1 = bf16[3,512,1024]{1,2,0:T(8,128)(2,1)} fusion(f32[3,514,1024]{1,2,0:T(8,128)S(1)} %maximum_convert_fusion.1, f32[3,1024]{1,0:T(4,128)S(1)} %get-tuple-element.115, f32[3,1024]{1,0:T(4,128)S(1)} %get-tuple-element.116, f32[3,1024]{1,0:T(4,128)S(1)} %bitcast.95), kind=kLoop, calls=%fused_computation.6 | loop fusion | flops 9437184 | bytes 22056960 | tf_op jit(solution)/shard_map/convert_element_type | solution.py:124
  235.1 4.6 %copy.63 = bf16[3,512,1024]{2,1,0:T(8,128)(2,1)} copy(bf16[3,512,1024]{1,2,0:T(8,128)(2,1)} %fusion.1) | data formatting | bytes 6291456
  (61 shorter events, 23.1 us)
Async XLA Ops:
  7.2 96.1 %all-gather.7.cloned.1.call-start = ((), (), s32[]{:S(2)}) async-start(), calls=%async_computation | async-start | bytes 4718592 | tf_op jit(solution)/shard_map/all_gather | solution.py:25
  8.0 10.5 %collective-permute-start = (bf16[3,2,1024]{2,1,0:T(2,128)(2,1)S(1)}, bf16[3,2,1024]{2,1,0:T(2,128)(2,1)S(1)}, u32[]{:S(2)}, u32[]{:S(2)}) collective-permute-start(bf16[3,2,1024]{2,1,0:T(2,128)(2,1)S(1)} %slice.46), channel_id=1, source_target_pairs={{0,4},{4,8},{8,12},{12,16},{16,20},{20,24},{24,28},{1,5},{5,9},{9,... | collective-permute-start | bytes 36872 | tf_op jit(solution)/shard_map/ppermute | solution.py:18
  28.5 3.7 %copy-start.2 = (bf16[1,512,1024]{1,2,0:T(8,128)(2,1)}, bf16[1,512,1024]{1,2,0:T(8,128)(2,1)S(1)}, u32[]{:S(2)}) copy-start(bf16[1,512,1024]{1,2,0:T(8,128)(2,1)S(1)} %get-tuple-element.103) | copy-start | bytes 3145732
  28.5 75.9 %copy-start.4 = (bf16[1,512,1024]{1,2,0:T(8,128)(2,1)}, bf16[1,512,1024]{1,2,0:T(8,128)(2,1)S(1)}, u32[]{:S(2)}) copy-start(bf16[1,512,1024]{1,2,0:T(8,128)(2,1)S(1)} %get-tuple-element.104) | copy-start | bytes 3145732
  30.0 178.7 %all-gather.9.cloned.1.call-start = ((), (), s32[]{:S(2)}) async-start(), calls=%async_computation.1 | async-start | bytes 4718592 | tf_op jit(solution)/shard_map/all_gather | solution.py:25
  30.1 0.7 copy-start.11
  32.2 2.0 copy-start
  103.3 1.0 copy-start.10
  104.4 5.3 %copy-start.12 = (f32[1024]{0:T(1024)S(1)}, f32[1024]{0:T(1024)}, u32[]{:S(2)}) copy-start(f32[1024]{0:T(1024)} %param.10) | copy-start | bytes 12292
  129.5 2.4 copy-start.3
  132.0 2.9 %copy-start.1 = (bf16[8,512,512]{2,1,0:T(8,128)(2,1)S(1)}, bf16[8,512,512]{2,1,0:T(8,128)(2,1)}, u32[]{:S(2)}) copy-start(bf16[8,512,512]{2,1,0:T(8,128)(2,1)} %copy-done) | copy-start | bytes 12582916
  134.9 2.1 copy-start.5
  208.7 8.5 %copy-start.9 = (f32[8,128,128]{2,1,0:T(8,128)S(1)}, f32[8,128,128]{2,1,0:T(8,128)}, u32[]{:S(2)}) copy-start(f32[8,128,128]{2,1,0:T(8,128)} %fusion.15) | copy-start | bytes 1572868
  217.1 2.3 copy-start.8
  217.2 3.2 %copy-start.6 = (bf16[8,128,512]{2,1,0:T(8,128)(2,1)S(1)}, bf16[8,128,512]{2,1,0:T(8,128)(2,1)}, u32[]{:S(2)}) copy-start(bf16[8,128,512]{2,1,0:T(8,128)(2,1)} %add_convert_fusion.2) | copy-start | bytes 3145732
  219.5 1.0 copy-start.7
  220.9 5.6 %collective-permute-start.1 = (bf16[3,2,1024]{2,1,0:T(2,128)(2,1)S(1)}, bf16[3,2,1024]{2,1,0:T(2,128)(2,1)S(1)}, u32[]{:S(2)}, u32[]{:S(2)}) collective-permute-start(bf16[3,2,1024]{2,1,0:T(2,128)(2,1)S(1)} %copy.61), channel_id=1, source_target_pairs={{4,0},{8,4},{12,8},{16,12},{20,16},{24,20},{28,24},{5,1},{9,5},{13... | collective-permute-start | bytes 36872 | tf_op jit(solution)/shard_map/ppermute | solution.py:18
Sparse Core Ops, SparseCore 0:
  30.1 73.0 all-gather.6
  129.7 78.9 all-gather.8
